TPU v7x, 256 devices: a whole 4x4x8 slice. The times are simulated.
256 devices in a mesh: dp: 32 (over z, x), expert: 8 (over y, core).
Axes of the slice: x: 4, y: 4, z: 8, core: 2. Of those that a mesh axis runs over, the one named last changes fastest.
Arguments:
- grads: bfloat16 [32, 8, 2048, 1024], P('dp', 'expert'), may hold values from -100 to 100
- signs: int32 [8, 1024], P('expert'), may hold values from -1 to 1, as said below
- weights: bfloat16 [8, 2048, 1024], P('expert', 'dp'), may hold values from -4 to 4
- compensation: bfloat16 [8, 2048, 1024], P('expert', 'dp'), may hold values from -0.099609375 to 0.099609375
Outputs:
- new_weights: bfloat16 [8, 2048, 1024], P('expert')
- update_grad: float32 [8, 2048, 1024], P('expert', 'dp')
Inputs may be any that keep to these rules, and one draw needn't show every extreme that they name: `signs`: each entry is -1 or +1.
All inputs are finite; a program needn't handle non-finite values.
Results may differ from a plain program's by a relative error of at most 0.0018.
The roundings to bfloat16 on the way count: a program that leaves them out, or rounds other values in their place, can miss the bound.
Values may be sent and summed in bfloat16 or wider, within the bound.
A program may use at most 64 MiB of HBM per device.

v0:
```python
import functools
import math

import jax
import jax.numpy as jnp
from jax import lax
from jax.sharding import Mesh
from jax.sharding import PartitionSpec as P

DP = ("dp_0", "dp_1")
DP_EXPERT = ("dp_0", "dp_1", "expert_0", "expert_1")
EXPERT = ("expert_0", "expert_1")


clamp_level = 2.0
target_rms = 0.2
learn_rate = 0.02


def from_everyone(value, axis):
    copies = jnp.broadcast_to(value, (lax.axis_size(axis), *value.shape))
    return lax.all_to_all(copies, axis, split_axis=0, concat_axis=0, tiled=True)


def of_everyone(value, axis):
    return from_everyone(value, axis).max(axis=0)


def over_axes(value, axes):
    return functools.reduce(lax.psum, axes, value)


def gathered_by_axis(value, axes, dim):
    if not axes:
        return value
    nearer = lax.all_gather(value, axes[-1], axis=dim, tiled=True)
    return gathered_by_axis(nearer, axes[:-1], dim)


def hadamard(width):
    counter = lax.iota(jnp.int32, width)
    common = counter[:, None] & counter[None, :]
    parity = jnp.zeros((width, width), jnp.int32)
    for position in range(width.bit_length() - 1):
        parity = parity ^ common >> position & 1
    return (1 - 2 * parity).astype(jnp.float32)


def on_device(grads, signs, weights, compensation):
    width = grads.shape[3]
    local_grads = grads.reshape(grads.shape[2], width)
    replicas = lax.axis_size(DP)
    owned = local_grads.shape[0] // replicas
    inverse_root = 1.0 / math.sqrt(width)
    sign_row = signs.reshape(width).astype(jnp.float32)
    matrix = hadamard(width)
    forward = (sign_row[:, None] * matrix).astype(jnp.bfloat16)
    values = local_grads.astype(jnp.float32)
    rms = jnp.sqrt(jnp.mean(values * values, axis=1) + 1e-06)
    scale = of_everyone(rms, DP)
    source = jnp.dot(local_grads, forward, preferred_element_type=jnp.float32) * inverse_root
    levels_all = jnp.clip(source / scale[:, None], -clamp_level, clamp_level).astype(jnp.bfloat16)
    received = lax.all_to_all(
        levels_all.reshape(replicas, owned, width), DP, split_axis=0, concat_axis=0, tiled=True
    )
    total = jnp.sum(received.astype(jnp.float32), axis=0)
    own_scale = lax.dynamic_slice_in_dim(scale, lax.axis_index(DP) * owned, owned, 0)
    mean_rot = total * own_scale[:, None] / replicas
    local_squares = jnp.sum(mean_rot * mean_rot)
    unrot = (
        jnp.dot(
            mean_rot, matrix, precision=lax.Precision.HIGHEST, preferred_element_type=jnp.float32
        )
        * inverse_root
        * sign_row[None, :]
    )
    squares = over_axes(local_squares, DP_EXPERT)
    limit = target_rms * math.sqrt(owned * width * replicas * lax.axis_size(EXPERT))
    factor = limit / jnp.maximum(jnp.sqrt(squares), limit)
    update_grad = (unrot * factor).reshape(weights.shape)
    summed = weights.astype(jnp.float32) + (
        compensation.astype(jnp.float32) - learn_rate * update_grad
    )
    new_weights = summed.astype(jnp.bfloat16)
    gathered = gathered_by_axis(new_weights, DP, 1)
    return (gathered, update_grad)


def solution(mesh):
    split = Mesh(mesh.devices.reshape(8, 4, 4, 2), ("dp_0", "dp_1", "expert_0", "expert_1"))
    in_specs = (
        P(DP, EXPERT, None, None),
        P(EXPERT, None),
        P(EXPERT, DP, None),
        P(EXPERT, DP, None),
    )
    out_specs = (P(EXPERT, None, None), P(EXPERT, DP, None))
    return jax.shard_map(
        on_device, mesh=split, in_specs=in_specs, out_specs=out_specs, check_vma=False
    )
```

profile of v0, /device:TPU:8, one launch (start us, length us, event | category | flops | bytes accessed | tf_op | source)
XLA Modules:
  0.0 282.9 jit_solution(8464213056624999051)
XLA Ops:
  7.2 0.0 copy-start
  7.2 3.1 %multiply_reduce_fusion = f32[2048]{0:T(1024)S(1)} fusion(bf16[1,1,2048,1024]{3,2,1,0:T(8,128)(2,1)} %param.4), kind=kLoop, calls=%fused_computation.2 | loop fusion | flops 6289408 | bytes 4202496 | tf_op jit(solution)/shard_map/reduce_sum | solution.py:59
  10.3 0.8 broadcast_in_dim.2
  11.1 11.3 %all-to-all-start = ((f32[32,1,2048]{2,1,0:T(1,128)}), f32[32,1,2048]{2,1,0:T(1,128)S(1)}, u32[]{:S(2)}, u32[]{:S(2)}) async-start(f32[32,1,2048]{2,1,0:T(1,128)} %broadcast_in_dim.2), calls=%async_computation | async-start | bytes 524288 | tf_op jit(solution)/shard_map/all_to_all | solution.py:22
  22.4 0.0 copy-done
  22.5 12.8 %all-to-all-done = f32[32,1,2048]{2,1,0:T(1,128)S(1)} async-done(((f32[32,1,2048]{2,1,0:T(1,128)}), f32[32,1,2048]{2,1,0:T(1,128)S(1)}, u32[]{:S(2)}, u32[]{:S(2)}) %all-to-all-start) | async-done | bytes 262176 | tf_op jit(solution)/shard_map/all_to_all | solution.py:22
  35.2 0.2 reduce_max.9
  35.4 12.5 %fusion.3 = bf16[2048,1024]{0,1:T(8,128)(2,1)} fusion(f32[2048]{0:T(1024)S(1)} %reduce_max.9, bf16[1,1,2048,1024]{3,2,1,0:T(8,128)(2,1)} %param.4, f32[1024]{0:T(1024)S(1)} %bitcast.20), kind=kOutput, calls=%fused_computation.8 | convolution fusion | flops 4340056064 | bytes 8400896 | tf_op jit(solution)/shard_map/dot_general | solution.py:61
  47.9 6.4 %copy.9 = bf16[2048,1024]{1,0:T(8,128)(2,1)} copy(bf16[2048,1024]{0,1:T(8,128)(2,1)} %fusion.3) | data formatting | bytes 8388608 | tf_op jit(solution)/shard_map/convert_element_type | solution.py:62
  54.3 4.8 %all-to-all-start.1 = ((bf16[32,64,1024]{2,1,0:T(8,128)(2,1)}), bf16[32,64,1024]{2,1,0:T(8,128)(2,1)}, u32[]{:S(2)}, u32[]{:S(2)}) async-start(bf16[32,64,1024]{2,1,0:T(8,128)(2,1)} %bitcast.18), calls=%async_computation.1 | async-start | bytes 8388608 | tf_op jit(solution)/shard_map/all_to_all | solution.py:63
  59.1 0.0 copy-start.1
  59.2 0.0 copy-start.2
  59.2 0.0 all-gather.2.cloned.1.call-start
  59.2 0.1 dynamic_slice.3
  59.3 94.1 %all-to-all-done.1 = bf16[32,64,1024]{2,1,0:T(8,128)(2,1)} async-done(((bf16[32,64,1024]{2,1,0:T(8,128)(2,1)}), bf16[32,64,1024]{2,1,0:T(8,128)(2,1)}, u32[]{:S(2)}, u32[]{:S(2)}) %all-to-all-start.1) | async-done | bytes 4194336 | tf_op jit(solution)/shard_map/all_to_all | solution.py:63
  153.4 3.1 %convert_reduce_fusion = f32[64,1024]{1,0:T(8,128)S(1)} fusion(bf16[32,64,1024]{2,1,0:T(8,128)(2,1)} %all-to-all-done.1), kind=kLoop, calls=%fused_computation | loop fusion | flops 4128768 | bytes 4456448 | tf_op jit(solution)/shard_map/reduce_sum | solution.py:66
  156.6 0.7 multiply_reduce_fusion.1
  157.3 15.4 %psum.28 = f32[]{:T(128)} all-reduce(f32[]{:T(128)} %multiply_reduce_fusion.1), channel_id=1, replica_groups=mesh['dp_0'=8,'dp_1'=4,'expert_0'=4,'expert_1'=2] {'dp_0'}, use_global_device_ids=true, to_apply=%region_4.5 | all-reduce | flops 1 | bytes 8 | tf_op jit(solution)/shard_map/psum | solution.py:30
  172.7 11.0 %psum.29 = f32[]{:T(128)} all-reduce(f32[]{:T(128)} %psum.28), channel_id=1, replica_groups=mesh['dp_0'=8,'dp_1'=4,'expert_0'=4,'expert_1'=2] {'dp_1'}, use_global_device_ids=true, to_apply=%region_5.6 | all-reduce | flops 1 | bytes 8 | tf_op jit(solution)/shard_map/psum | solution.py:30
  183.7 9.3 %psum.30 = f32[]{:T(128)} all-reduce(f32[]{:T(128)} %psum.29), channel_id=1, replica_groups=mesh['dp_0'=8,'dp_1'=4,'expert_0'=4,'expert_1'=2] {'expert_0'}, use_global_device_ids=true, to_apply=%region_6.7 | all-reduce | flops 1 | bytes 8 | tf_op jit(solution)/shard_map/psum | solution.py:30
  193.0 3.1 %psum.31 = f32[]{:T(128)} all-reduce(f32[]{:T(128)} %psum.30), channel_id=1, replica_groups=mesh['dp_0'=8,'dp_1'=4,'expert_0'=4,'expert_1'=2] {'expert_1'}, use_global_device_ids=true, to_apply=%region_7.8 | all-reduce | flops 1 | bytes 8 | tf_op jit(solution)/shard_map/psum | solution.py:30
  196.8 0.0 copy-done.1
  196.8 0.0 copy-done.2
  196.8 8.0 %fusion.14 = (bf16[1,64,1024]{2,1,0:T(8,128)(2,1)S(1)}, f32[64,1024]{1,0:T(8,128)}) fusion(bf16[1,64,1024]{2,1,0:T(8,128)(2,1)S(1)} %copy-done.1, bf16[1,64,1024]{2,1,0:T(8,128)(2,1)S(1)} %copy-done.2, f32[]{:T(128)S(6)} %div.30, f32[1024]{0:T(1024)S(1)} %bitcast.19, f32[64,1024]{1,0:T(8,128)S(1)} %convert_reduce_fusion, f32[64]{0:T(128)S(1)} %dynamic_slice.3), kind=kOutput, calls=%fused_computation.14 | convolution fusion | flops 840564736 | bytes 921860 | tf_op jit(solution)/shard_map/dot_general | solution.py:71
  204.9 14.2 %all_gather.6 = bf16[1,256,1024]{2,1,0:T(8,128)(2,1)} all-gather(bf16[1,64,1024]{2,1,0:T(8,128)(2,1)S(1)} %get-tuple-element.2), channel_id=1, replica_groups=mesh['dp_0'=8,'dp_1'=4,'expert_0'=4,'expert_1'=2] {'dp_1'}, dimensions={1}, use_global_device_ids=true | all-gather | bytes 655360 | tf_op jit(solution)/shard_map/all_gather | solution.py:36
  219.1 0.0 all-gather.2.cloned.1.call-update
  219.1 52.3 %all-gather.2.cloned.1.call-done = bf16[1,2048,1024]{2,1,0:T(8,128)(2,1)} async-done(((bf16[1,256,1024]{2,1,0:T(8,128)(2,1)}), bf16[1,2048,1024]{2,1,0:T(8,128)(2,1)}) %all-gather.2.cloned.1.call-update) | async-done | bytes 4194320 | tf_op jit(solution)/shard_map/all_gather | solution.py:36
  271.4 4.6 %copy.12 = bf16[1,2048,1024]{2,1,0:T(8,128)(2,1)} copy(bf16[1,2048,1024]{2,1,0:T(8,128)(2,1)} %all-gather.2.cloned.1.call-done) | data formatting | bytes 8388608
  (3 shorter events, 0.0 us)
Async XLA Ops:
  7.2 15.3 %copy-start = (s32[1,1024]{1,0:T(1,128)S(1)}, s32[1,1024]{1,0:T(1,128)}, u32[]{:S(2)}) copy-start(s32[1,1024]{1,0:T(1,128)} %param.5) | copy-start | bytes 12292
  11.1 24.1 %all-to-all-start = ((f32[32,1,2048]{2,1,0:T(1,128)}), f32[32,1,2048]{2,1,0:T(1,128)S(1)}, u32[]{:S(2)}, u32[]{:S(2)}) async-start(f32[32,1,2048]{2,1,0:T(1,128)} %broadcast_in_dim.2), calls=%async_computation | async-start | bytes 524288 | tf_op jit(solution)/shard_map/all_to_all | solution.py:22
  54.3 99.1 %all-to-all-start.1 = ((bf16[32,64,1024]{2,1,0:T(8,128)(2,1)}), bf16[32,64,1024]{2,1,0:T(8,128)(2,1)}, u32[]{:S(2)}, u32[]{:S(2)}) async-start(bf16[32,64,1024]{2,1,0:T(8,128)(2,1)} %bitcast.18), calls=%async_computation.1 | async-start | bytes 8388608 | tf_op jit(solution)/shard_map/all_to_all | solution.py:63
  59.1 137.7 %copy-start.1 = (bf16[1,64,1024]{2,1,0:T(8,128)(2,1)S(1)}, bf16[1,64,1024]{2,1,0:T(8,128)(2,1)}, u32[]{:S(2)}) copy-start(bf16[1,64,1024]{2,1,0:T(8,128)(2,1)} %param.7) | copy-start | bytes 393220
  59.2 137.7 %copy-start.2 = (bf16[1,64,1024]{2,1,0:T(8,128)(2,1)S(1)}, bf16[1,64,1024]{2,1,0:T(8,128)(2,1)}, u32[]{:S(2)}) copy-start(bf16[1,64,1024]{2,1,0:T(8,128)(2,1)} %param.6) | copy-start | bytes 393220
  59.2 212.2 %all-gather.2.cloned.1.call-start = ((), (), s32[]{:S(2)}) async-start(), calls=%async_computation.2 | async-start | bytes 4718592 | tf_op jit(solution)/shard_map/all_gather | solution.py:36
Sparse Core Ops, SparseCore 0:
  219.2 52.1 all-gather.1
where the time goes:
time: 284 us; the launch traced here: 283 us
  waiting for transfers between devices  159 us (56%)
  blocking collectives  53 us (19%)
  matrix products  20.5 us (7%)
  starting transfers between devices  16.2 us (6%)
  between operations  14.9 us (5%)
  local copies, waits for them, and re-layouts  12 us (4%)
  other arithmetic  7.14 us (3%)
    all_to_all x1, waiting for transfers between devices, on_device(): lax.all_to_all(levels_all.reshape(replicas, owned, width), DP, split_axis...  94.1 us
    all_gather x1, waiting for transfers between devices, gathered_by_axis(): nearer = lax.all_gather(value, axes[-1], axis=dim, tiled=True)  52.3 us
    psum x4, blocking collectives, over_axes(): return functools.reduce(lax.psum, axes, value)  38.8 us
    all_gather x1, blocking collectives, gathered_by_axis(): nearer = lax.all_gather(value, axes[-1], axis=dim, tiled=True)  14.2 us
    all_to_all x1, waiting for transfers between devices, from_everyone(): return lax.all_to_all(copies, axis, split_axis=0, concat_axis=0, tiled=True)  12.8 us
    dot_general x1, matrix products, on_device(): jnp.dot(local_grads, forward, preferred_element_type=jnp.float32)  12.5 us
    all_to_all x1, starting transfers between devices, from_everyone(): return lax.all_to_all(copies, axis, split_axis=0, concat_axis=0, tiled=True)  11.3 us
    dot_general x1, matrix products, on_device(): jnp.dot(mean_rot, matrix, precision=lax.Precision.HIGHEST, preferred_elem...  8.03 us
  transfers between devices with their start and end apart: 3, of which 3 were waited for; matrix products, arithmetic and copies ran while one was open for 0% of the time, Pallas kernels for 0%

commit v1 on v0

v1 whole, which is shorter than its diff:
```python
import heapq
import math

import jax
import jax.numpy as jnp
from jax import lax
from jax.experimental import pallas as pl
from jax.experimental.pallas import tpu as pltpu
from jax.sharding import PartitionSpec as P

MESH = pl.DeviceIdType.MESH
F32 = jnp.float32
BF16 = jnp.bfloat16

clamp_level = 2.0
target_rms = 0.2
learn_rate = 0.02

Z, X, Y, CORES = 8, 4, 4, 2
ROWS, WIDTH, OWNED = 2048, 1024, 64
GROUP = ROWS // Z
SUB = 256
HALF = OWNED // 2
TILE = 16
R1 = 24
ORDER = (4, 3, -3, 2, -2, 1, -1, 0)
NX, NZ, NE = X - 1, Z - 1, Y * CORES - 1


def gather_plan():
    copies = {}

    def add(name, link, lo, hi, after, block):
        copies[name] = dict(link=link, lo=lo, hi=hi, after=after, block=block)

    def z_chain(tag, dx, lo, hi, cut, after):
        for sign, link in ((1, "z+"), (-1, "z-")):
            prev = after
            for k in range(4):
                a, b = lo, hi
                if k == 3:
                    a, b = (lo, cut) if sign == 1 else (cut, hi)
                if b > a:
                    add((tag, link, k), link, a, b, prev, (-sign * (k + 1), dx))
                prev = ((tag, link, k),)

    def x_step(tag, dz, lo, hi, cut, after):
        for sign, link in ((1, "x+"), (-1, "x-")):
            add((tag, link, 0), link, lo, hi, after, (dz, -sign))
            a, b = (lo, cut) if sign == 1 else (cut, hi)
            add((tag, link, 1), link, a, b, ((tag, link, 0),), (dz, -2 * sign))

    x_step("p1x", 0, 0, R1, 16, ())
    z_chain("p2z", 0, R1, OWNED, R1 + 24, ())
    x_step("p2x0", 0, R1, OWNED, R1 + 24, ())
    z_chain("p1z0", 0, 0, R1, 8, ())
    z_chain("p1z1", -1, 0, R1, 8, (("p1x", "x+", 0),))
    z_chain("p1z-1", 1, 0, R1, 8, (("p1x", "x-", 0),))
    z_chain("p1z2", 2, 0, R1, 8, (("p1x", "x+", 1), ("p1x", "x-", 1)))
    for k in range(4):
        cut = R1 + (16 if k % 2 else 24)
        if k < 3:
            x_step(f"p2x{k + 1}", -(k + 1), R1, OWNED, cut, (("p2z", "z+", k),))
            x_step(f"p2x{-k - 1}", k + 1, R1, OWNED, OWNED + R1 - cut, (("p2z", "z-", k),))
        else:
            x_step("p2x4", 4, R1, OWNED, cut, (("p2z", "z+", 3), ("p2z", "z-", 3)))

    per_row, hop = WIDTH * 2 / 45e3, 1.7
    free = {link: 0.0 for link in ("x+", "x-", "z+", "z-")}
    events, done, order = [], set(), []
    started = set()

    def start_ready(now, current):
        names = []
        for name, c in copies.items():
            if name not in started and all(a in done for a in c["after"]):
                started.add(name)
                begin = max(now, free[c["link"]])
                end = begin + (c["hi"] - c["lo"]) * per_row
                free[c["link"]] = end
                heapq.heappush(events, (end + hop, len(started), name))
                names.append(name)
        order.append((current, names))

    start_ready(0.0, None)
    last = 0.0
    while events:
        last, _, name = heapq.heappop(events)
        done.add(name)
        start_ready(last, name)
    return copies, order, last


def kernel_body(
    grads, signs, weights, comp, out, upd,
    gbuf, rot, quant, left_in, right_in, far_in, left_relay, right_relay,
    zsend, zrecv, total, hmat,
    cbuf, cx, cz, sbuf, se, sx, sz,
    load_sem, small_send, small_recv, rs_send, rs_recv, zring_send, zring_recv, ag_send, ag_recv,
):
    dp = lax.axis_index("dp")
    expert = lax.axis_index("expert")
    z, x = dp // X, lax.rem(dp, X)
    inverse_root = 1.0 / math.sqrt(WIDTH)

    def at(dz, dx, de=0):
        other_z = lax.rem(z + (dz + Z), Z)
        other_x = lax.rem(x + (dx + X), X)
        other_e = lax.rem(expert + de, Y * CORES) if de else expert
        return (other_z * X + other_x, other_e)

    def remote(src, dst, send, recv, where):
        return pltpu.make_async_remote_copy(
            src_ref=src, dst_ref=dst, send_sem=send, recv_sem=recv,
            device_id=where, device_id_type=MESH,
        )

    pending = []

    def send(src, dst, ssem, rsem, where):
        copy = remote(src, dst, ssem, rsem, where)
        copy.start()
        pending.append(copy)

    def wait_for(dst, ssem, rsem):
        remote(dst, dst, ssem, rsem, at(0, 1)).wait_recv()

    barrier = pltpu.get_barrier_semaphore()
    peers = [at(0, d) for d in range(1, X)]
    peers += [at(d, 0) for d in range(1, Z)]
    peers += [at(0, 0, d) for d in range(1, Y * CORES)]
    for peer in peers:
        pl.semaphore_signal(barrier, inc=1, device_id=peer, device_id_type=MESH)

    loads = []
    for g in range(Z):
        rows = pl.ds(g * GROUP, GROUP)
        copy = pltpu.make_async_copy(grads.at[rows, :], gbuf.at[rows, :], load_sem.at[g])
        copy.start()
        loads.append(copy)

    common = lax.broadcasted_iota(jnp.int32, (SUB, SUB), 0) & lax.broadcasted_iota(
        jnp.int32, (SUB, SUB), 1
    )
    for shift in (4, 2, 1):
        common = common ^ (common >> shift)
    plain = (1 - 2 * (common & 1)).astype(F32)
    hmat[4] = plain.astype(BF16)
    sign_row = signs[...].astype(F32)
    for a in range(4):
        hmat[a] = (plain * sign_row[:, a * SUB : (a + 1) * SUB]).astype(BF16)

    lane = lax.broadcasted_iota(jnp.int32, (TILE, 128), 1)

    squares = jnp.zeros((TILE, 128), F32)
    for g in range(Z):
        loads[g].wait()

        def measure(i, acc, g=g):
            tile = gbuf[pl.ds(pl.multiple_of(g * GROUP + i * TILE, TILE), TILE), :].astype(F32)
            tile = tile * tile
            part = tile[:, 0:128]
            for a in range(1, WIDTH // 128):
                part = part + tile[:, a * 128 : (a + 1) * 128]
            row = jnp.sum(part, axis=1, keepdims=True)
            return jnp.where(lane == g * (GROUP // TILE) + i, row, acc)

        squares = lax.fori_loop(0, GROUP // TILE, measure, squares, unroll=4)
    cbuf[0] = squares

    pl.semaphore_wait(barrier, len(peers))

    def rotate(g, _):
        rows = pl.ds(pl.multiple_of(g * GROUP, GROUP), GROUP)
        for a in range(4):
            cols = slice(a * SUB, (a + 1) * SUB)
            rot[rows, cols] = lax.dot_general(
                gbuf[rows, cols], hmat[a], (((1,), (1,)), ((), ())), preferred_element_type=F32
            )
        return 0

    for d in range(1, X):
        send(cbuf.at[0], cx.at[d - 1], small_send.at[d - 1], small_recv.at[d - 1], at(0, d))
    lax.fori_loop(0, 3, rotate, 0)
    best = cbuf[0]
    for d in range(1, X):
        wait_for(cx.at[d - 1], small_send.at[d - 1], small_recv.at[d - 1])
        best = jnp.maximum(best, cx[d - 1])
    cbuf[1] = best
    for d in range(1, Z):
        k = NX + d - 1
        send(cbuf.at[1], cz.at[d - 1], small_send.at[k], small_recv.at[k], at(d, 0))
    lax.fori_loop(3, Z, rotate, 0)
    for d in range(1, Z):
        k = NX + d - 1
        wait_for(cz.at[d - 1], small_send.at[k], small_recv.at[k])
        best = jnp.maximum(best, cz[d - 1])
    scale = jnp.sqrt(best * (1.0 / WIDTH) + 1e-06)
    cbuf[2] = scale
    cbuf[3] = inverse_root / scale

    def row_values(index, which):
        return jnp.sum(jnp.where(lane == index, cbuf[which], 0.0), axis=1, keepdims=True)

    def butterfly(parts):
        u0, u1 = parts[0] + parts[1], parts[0] - parts[1]
        u2, u3 = parts[2] + parts[3], parts[2] - parts[3]
        return u0 + u2, u1 + u3, u0 - u2, u1 - u3

    def quantize(zt):
        def step(i, _):
            index = zt * (GROUP // TILE) + i
            rows = pl.ds(pl.multiple_of(index * TILE, TILE), TILE)
            inverse = row_values(index, 3)
            parts = [rot[rows, a * SUB : (a + 1) * SUB] for a in range(4)]
            for a, part in enumerate(butterfly(parts)):
                level = jnp.clip(part * inverse, -clamp_level, clamp_level)
                quant[rows, a * SUB : (a + 1) * SUB] = level.astype(BF16)
            return 0

        lax.fori_loop(0, GROUP // TILE, step, 0, unroll=2)

    def owner_z(d):
        return lax.rem(z + (d + Z), Z)

    def quant_rows(zt, dx, lo, n):
        first = zt * GROUP + lax.rem(x + (dx + X), X) * OWNED + lo
        return quant.at[pl.ds(pl.multiple_of(first, TILE), n), :]

    def send_group(i):
        zt = owner_z(ORDER[i])
        quantize(zt)
        s, r = rs_send.at[i], rs_recv.at[i]
        send(quant_rows(zt, 2, 0, HALF), left_relay.at[i], s.at[0], r.at[0], at(0, 1))
        send(quant_rows(zt, 2, HALF, HALF), right_relay.at[i], s.at[1], r.at[1], at(0, -1))
        send(quant_rows(zt, 1, 0, OWNED), left_in.at[i], s.at[2], r.at[2], at(0, 1))
        send(quant_rows(zt, -1, 0, OWNED), right_in.at[i], s.at[3], r.at[3], at(0, -1))

    def relay_group(i):
        s, r = rs_send.at[i], rs_recv.at[i]
        low, high = pl.ds(0, HALF), pl.ds(HALF, HALF)
        wait_for(left_relay.at[i], s.at[0], r.at[0])
        send(left_relay.at[i], far_in.at[i, low, :], s.at[4], r.at[4], at(0, 1))
        wait_for(right_relay.at[i], s.at[1], r.at[1])
        send(right_relay.at[i], far_in.at[i, high, :], s.at[5], r.at[5], at(0, -1))

    def zsem(kind, dirn, d):
        return kind.at[dirn, d]

    def sum_group(i):
        d = ORDER[i]
        zt = owner_z(d)
        s, r = rs_send.at[i], rs_recv.at[i]
        low, high = pl.ds(0, HALF), pl.ds(HALF, HALF)
        wait_for(left_in.at[i], s.at[2], r.at[2])
        wait_for(right_in.at[i], s.at[3], r.at[3])
        wait_for(far_in.at[i, low, :], s.at[4], r.at[4])
        wait_for(far_in.at[i, high, :], s.at[5], r.at[5])
        base = zt * GROUP + x * OWNED

        def here(t):
            rows = pl.ds(pl.multiple_of(t * TILE, TILE), TILE)
            own = quant[pl.ds(pl.multiple_of(base + t * TILE, TILE), TILE), :].astype(F32)
            near = left_in[i, rows, :].astype(F32) + right_in[i, rows, :].astype(F32)
            return rows, own + near + far_in[i, rows, :].astype(F32)

        def run(lo, hi, dst, extra):
            def step(t, _):
                rows, value = here(t)
                for ref in extra:
                    value = value + ref[rows, :]
                dst[rows, :] = value
                return 0

            lax.fori_loop(lo // TILE, hi // TILE, step, 0)

        def pass_on(dirn, d, rows):
            k = d - 1
            send(
                zsend.at[dirn, k, rows, :], zrecv.at[dirn, k, rows, :],
                zring_send.at[dirn, k], zring_recv.at[dirn, k], at(1 if dirn == 0 else -1, 0),
            )

        def arrived(dirn, k, rows):
            wait_for(zrecv.at[dirn, k, rows, :], zring_send.at[dirn, k], zring_recv.at[dirn, k])

        every = pl.ds(0, OWNED)
        if d == 4:
            run(0, HALF, zsend.at[0, 3], ())
            run(HALF, OWNED, zsend.at[1, 3], ())
            pass_on(0, 4, low)
            pass_on(1, 4, high)
        elif d == 0:
            arrived(0, 0, every)
            arrived(1, 0, every)
            run(0, OWNED, total, (zrecv.at[0, 0], zrecv.at[1, 0]))
        else:
            dirn, k = (0, d) if d > 0 else (1, -d)
            slot, kept = zsend.at[dirn, k - 1], zrecv.at[dirn, k]
            if k == 3:
                arrived(dirn, 3, low if dirn == 0 else high)
                run(0, HALF, slot, (kept,) if dirn == 0 else ())
                run(HALF, OWNED, slot, (kept,) if dirn == 1 else ())
            else:
                arrived(dirn, k, every)
                run(0, OWNED, slot, (kept,))
            pass_on(dirn, k, every)

    for step in range(Z + 2):
        if step < Z:
            send_group(step)
        if 1 <= step <= Z:
            relay_group(step - 1)
        if step >= 2:
            sum_group(step - 2)

    def scale_rows(t, acc):
        rows = pl.ds(pl.multiple_of(t * TILE, TILE), TILE)
        mean = total[rows, :] * row_values(dp * (OWNED // TILE) + t, 2) * (1.0 / (Z * X))
        total[rows, :] = mean
        mean = mean * mean
        part = mean[:, 0:128]
        for a in range(1, WIDTH // 128):
            part = part + mean[:, a * 128 : (a + 1) * 128]
        return acc + part[0:8] + part[8:16]

    sbuf[0] = lax.fori_loop(0, OWNED // TILE, scale_rows, jnp.zeros((8, 128), F32))
    first = NX + NZ
    for d in range(1, NE + 1):
        k = first + d - 1
        send(sbuf.at[0], se.at[d - 1], small_send.at[k], small_recv.at[k], at(0, 0, d))

    parts = butterfly([total[:, a * SUB : (a + 1) * SUB] for a in range(4)])
    for a, part in enumerate(parts):
        high = part.astype(BF16)
        rest = part - high.astype(F32)
        middle = rest.astype(BF16)
        low = (rest - middle.astype(F32)).astype(BF16)
        value = jnp.dot(low, hmat[4], preferred_element_type=F32)
        value = value + jnp.dot(middle, hmat[4], preferred_element_type=F32)
        value = value + jnp.dot(high, hmat[4], preferred_element_type=F32)
        cols = slice(a * SUB, (a + 1) * SUB)
        upd[:, cols] = value * (sign_row[:, cols] * inverse_root)

    def reduce_over(source, slots, count, base, dst):
        value = sbuf[source]
        for d in range(1, count + 1):
            k = base + d - 1
            wait_for(slots.at[d - 1], small_send.at[k], small_recv.at[k])
            value = value + slots[d - 1]
        if dst is not None:
            sbuf[dst] = value
        return value

    reduce_over(0, se, NE, first, 1)
    first += NE
    for d in range(1, X):
        k = first + d - 1
        send(sbuf.at[1], sx.at[d - 1], small_send.at[k], small_recv.at[k], at(0, d))
    reduce_over(1, sx, NX, first, 2)
    first += NX
    for d in range(1, Z):
        k = first + d - 1
        send(sbuf.at[2], sz.at[d - 1], small_send.at[k], small_recv.at[k], at(d, 0))
    vector = reduce_over(2, sz, NZ, first, None)
    sum_squares = jnp.sum(jnp.sum(vector, axis=1, keepdims=True), axis=0, keepdims=True)
    limit = target_rms * math.sqrt(ROWS * WIDTH * Y * CORES)
    factor = limit / jnp.maximum(jnp.sqrt(sum_squares), limit)

    def update(t, _):
        rows = pl.ds(pl.multiple_of(t * TILE, TILE), TILE)
        grad = upd[rows, :] * factor
        upd[rows, :] = grad
        new = weights[rows, :].astype(F32) + (comp[rows, :].astype(F32) - learn_rate * grad)
        out[z, x, rows, :] = new.astype(BF16)
        return 0

    lax.fori_loop(0, OWNED // TILE, update, 0)

    copies, order, _ = gather_plan()
    number = {name: k for k, name in enumerate(copies)}
    steps = {"z+": (1, 0), "z-": (-1, 0), "x+": (0, 1), "x-": (0, -1)}

    def view(dz, dx, c):
        rows = pl.ds(c["lo"], c["hi"] - c["lo"])
        other_x = lax.rem(x + (dx + X), X)
        return out.at[lax.rem(z + (dz + Z), Z), other_x, rows, :]

    for arrival, names in order:
        if arrival is not None:
            c, k = copies[arrival], number[arrival]
            wait_for(view(*c["block"], c), ag_send.at[k], ag_recv.at[k])
        for name in names:
            c, k = copies[name], number[name]
            dz, dx = steps[c["link"]]
            block = view(c["block"][0] + dz, c["block"][1] + dx, c)
            send(block, block, ag_send.at[k], ag_recv.at[k], at(dz, dx))

    for copy in pending:
        copy.wait_send()


def on_device(grads, signs, weights, comp):
    copies, _, _ = gather_plan()
    vmem = pl.BlockSpec(memory_space=pltpu.VMEM)
    small = NX + NZ + NE + NX + NZ
    dma = pltpu.SemaphoreType.DMA
    out, upd = pl.pallas_call(
        kernel_body,
        out_shape=(
            pltpu.VMEM((Z, X, OWNED, WIDTH), BF16),
            pltpu.VMEM((OWNED, WIDTH), F32),
        ),
        in_specs=[pl.BlockSpec(memory_space=pl.ANY), vmem, vmem, vmem],
        out_specs=(vmem, vmem),
        scratch_shapes=[
            pltpu.VMEM((ROWS, WIDTH), BF16),
            pltpu.VMEM((ROWS, WIDTH), F32),
            pltpu.VMEM((ROWS, WIDTH), BF16),
            pltpu.VMEM((Z, OWNED, WIDTH), BF16),
            pltpu.VMEM((Z, OWNED, WIDTH), BF16),
            pltpu.VMEM((Z, OWNED, WIDTH), BF16),
            pltpu.VMEM((Z, HALF, WIDTH), BF16),
            pltpu.VMEM((Z, HALF, WIDTH), BF16),
            pltpu.VMEM((2, 4, OWNED, WIDTH), F32),
            pltpu.VMEM((2, 4, OWNED, WIDTH), F32),
            pltpu.VMEM((OWNED, WIDTH), F32),
            pltpu.VMEM((5, SUB, SUB), BF16),
            pltpu.VMEM((4, TILE, 128), F32),
            pltpu.VMEM((NX, TILE, 128), F32),
            pltpu.VMEM((NZ, TILE, 128), F32),
            pltpu.VMEM((3, 8, 128), F32),
            pltpu.VMEM((NE, 8, 128), F32),
            pltpu.VMEM((NX, 8, 128), F32),
            pltpu.VMEM((NZ, 8, 128), F32),
            dma((Z,)),
            dma((small,)),
            dma((small,)),
            dma((Z, 6)),
            dma((Z, 6)),
            dma((2, 4)),
            dma((2, 4)),
            dma((len(copies),)),
            dma((len(copies),)),
        ],
        compiler_params=pltpu.CompilerParams(
            collective_id=0, has_side_effects=True, vmem_limit_bytes=48 * 1024 * 1024
        ),
    )(
        grads.reshape(ROWS, WIDTH),
        signs.reshape(1, WIDTH),
        weights.reshape(OWNED, WIDTH),
        comp.reshape(OWNED, WIDTH),
    )
    return out.reshape(1, ROWS, WIDTH), upd.reshape(1, OWNED, WIDTH)


def solution(mesh):
    in_specs = (
        P("dp", "expert", None, None),
        P("expert", None),
        P("expert", "dp", None),
        P("expert", "dp", None),
    )
    out_specs = (P("expert", None, None), P("expert", "dp", None))
    return jax.shard_map(
        on_device, mesh=mesh, in_specs=in_specs, out_specs=out_specs, check_vma=False
    )
```

time: 284 us -> 122 us (0.43)
  waiting for transfers between devices: 159 us -> 0 us
  Pallas kernels: 0 us -> 116 us
  blocking collectives: 53 us -> 0 us
  matrix products: 20.5 us -> 0 us
  starting transfers between devices: 16.2 us -> 0 us
  between operations: 14.9 us -> 0.65 us
  other arithmetic: 7.14 us -> 0 us
  local copies, waits for them, and re-layouts: 12 us -> 5.21 us
    pallas_call x0 -> x1, Pallas kernels: none -> 116 us  [on_device(): pl.pallas_call(kernel_body, out_shape=(pltpu.VMEM((Z, X, OWNED, WIDTH), B...]
    all_to_all x2 -> x0, waiting for transfers between devices: 107 us -> none  [the longest x1 94.1 us: on_device(): lax.all_to_all(levels_all.reshape(replicas, owned, width), DP, split_axis...]
    all_gather x1 -> x0, waiting for transfers between devices: 52.3 us -> none  [gathered_by_axis(): nearer = lax.all_gather(value, axes[-1], axis=dim, tiled=True)]
    psum x4 -> x0, blocking collectives: 38.8 us -> none  [over_axes(): return functools.reduce(lax.psum, axes, value)]
    dot_general x2 -> x0, matrix products: 20.5 us -> none  [the longest x1 12.5 us: on_device(): jnp.dot(local_grads, forward, preferred_element_type=jnp.float32)]
    all_to_all x2 -> x0, starting transfers between devices: 16.2 us -> none  [the longest x1 11.3 us: from_everyone(): return lax.all_to_all(copies, axis, split_axis=0, concat_axis=0, tiled=True)]
    all_gather x1 -> x0, blocking collectives: 14.2 us -> none  [gathered_by_axis(): nearer = lax.all_gather(value, axes[-1], axis=dim, tiled=True)]
    reduce_sum x3 -> x0, other arithmetic: 6.96 us -> none  [the longest x1 3.14 us: on_device(): total = jnp.sum(received.astype(jnp.float32), axis=0)]
  transfers between devices with their start and end apart: 3 -> 0, of which waited for: 3 -> 0; matrix products, arithmetic and copies ran while one was open for 0% -> 0% of each run, Pallas kernels for 0% -> 0%
where the time goes in v1:
time: 122 us; the launch traced here: 121 us
  Pallas kernels  116 us (95%)
  local copies, waits for them, and re-layouts  5.21 us (4%)
    pallas_call x1, Pallas kernels, on_device(): pl.pallas_call(kernel_body, out_shape=(pltpu.VMEM((Z, X, OWNED, WIDTH), B...  116 us
    unnamed x8, local copies, waits for them, and re-layouts  5.21 us

profile of v1, /device:TPU:8, one launch (start us, length us, event | category | flops | bytes accessed | tf_op | source)
XLA Modules:
  0.0 121.4 jit_solution(9670884843795615195)
XLA Ops:
  0.6 0.0 copy-start
  0.6 0.9 copy-done
  1.5 0.0 copy-start.1
  1.5 0.9 copy-done.1
  2.4 0.0 copy-start.2
  2.4 0.7 copy-done.2
  3.1 115.6 %shard_map.59 = (bf16[8,4,64,1024]{3,2,1,0:T(8,128)(2,1)S(1)}, f32[64,1024]{1,0:T(8,128)S(1)}) custom-call(bf16[2048,1024]{1,0:T(8,128)(2,1)} %bitcast.9, s32[1,1024]{1,0:T(1,128)S(1)} %copy-done.2, bf16[64,1024]{1,0:T(8,128)(2,1)S(1)} %bitcast.7, bf16[64,1024]{1,0:T(8,128)(2,1)S(1)} %bitcast.8), custom_call_target="tpu_custom_call" | custom-call | tf_op jit(solution)/shard_map/pallas_call | solution.py:408
  118.7 2.0 %copy.8 = bf16[1,2048,1024]{2,1,0:T(8,128)(2,1)} copy(bf16[1,2048,1024]{2,1,0:T(8,128)(2,1)S(1)} %bitcast.5) | data formatting | bytes 8388608
  120.7 0.7 copy.9
Async XLA Ops:
  0.6 0.9 copy-start
  1.5 0.9 copy-start.1
  2.4 0.7 copy-start.2
